TPU v7x, 256 devices: a whole 4x4x8 slice. The times are simulated.
256 devices in a mesh: group: 8 (over y, core), leaf: 32 (over z, x).
Axes of the slice: x: 4, y: 4, z: 8, core: 2. Of those that a mesh axis runs over, the one named last changes fastest.
Arguments:
- points: float32 [3, 524288], P(None, ('group', 'leaf')), may hold values from 0 to 1
- rhs: float32 [16, 524288], P(None, ('group', 'leaf')), may hold values from -0.5 to 0.5
- counts: int32 [4096], P(('group', 'leaf')), may hold values from 32 to 128
- basis: float32 [4096, 128, 32], P(('group', 'leaf')), may hold values from -1 to 1
- leaf_geom: float32 [4096, 4], P(('group', 'leaf')), may hold values from 0.05 to 1
- leaf_partners: int32 [4096, 16], P(('group', 'leaf')), may hold values from -16 to 16, as said below
- leaf_middle_owner: int32 [256, 16], P(('group', 'leaf')), may hold values from 0 to 7, never falling along the last dimension, each value on 1 to 4 neighbouring positions
- leaf_basis_transfer: float32 [4096, 32, 32], P(('group', 'leaf')), may hold values from -1 to 1
- mid_geom: float32 [2048, 4], P(('group', 'leaf')), may hold values from 0.05 to 1
- mid_parent: int32 [8, 256], P('group', 'leaf'), may hold values from 0 to 15, never falling along the last dimension, each value on 1 to 32 neighbouring positions
- mid_transfer: float32 [2048, 32, 32], P(('group', 'leaf')), may hold values from -1 to 1
- mid_peers: int32 [2048, 8], P(('group', 'leaf')), may hold values from 0 to 31, all different within a row; in each aligned block of 8 rows (0 to 7, 8 to 15, ...) at most 4 rows name the same one
- mid_slots: int32 [2048, 8], P(('group', 'leaf')), may hold values from 0 to 7
- top_geom: float32 [128, 4], P('group'), may hold values from 0.05 to 1
- top_offsets: int32 [128, 16], P('group'), may hold values from 1 to 127
Outputs:
- product: float32 [16, 524288], P(None, ('group', 'leaf'))
Inputs may be any that keep to these rules, and one draw needn't show every extreme that they name: `leaf_partners`: column 0 is 0. Every partner leaf lies in the same group, at most 16 leaves away. `mid_peers`: over the rows of one device, no device is named more than 4 times, and some device is named exactly 4 times; the names in a row differ. `leaf_middle_owner`: never falling along a row. `mid_parent`: never falling along a row.
All inputs are finite; a program needn't handle non-finite values.
Results may differ from a plain program's by a relative error of at most 0.00013.
Values sent between devices are 32-bit elements; how exact they have to be, the bound alone decides.
A program may use at most 64 MiB of HBM per device.

v0:
```python
import jax
import jax.numpy as jnp
from jax import lax
from jax.sharding import PartitionSpec as P

PTS = 128
RANK = 32
RHS = 16
TOP = 16
NEAR = 8
REACH = 16
exact_product = lax.Precision.HIGHEST
root_three = 1.7320508075688772
length_scale = 0.5


def extended(block, sides, width):
    for axis, dim in sides:
        count = lax.axis_size(axis)
        forward = [(i, i + 1) for i in range(count - 1)]
        backward = [(target, source) for source, target in forward]
        low = lax.ppermute(
            lax.slice_in_dim(block, block.shape[dim] - width, None, axis=dim), axis, forward
        )
        high = lax.ppermute(lax.slice_in_dim(block, 0, width, axis=dim), axis, backward)
        block = jnp.concatenate([low, block, high], axis=dim)
    return block


def node_table():
    indices = jnp.arange(RANK, dtype=jnp.int32)
    layers = []
    for axis_number in range(3):
        spread = (indices * (2 * axis_number + 3) % RANK).astype(jnp.float32)
        layers.append(jnp.cos(jnp.pi * (spread + 0.5) / RANK))
    return jnp.stack(layers)


def place_nodes(geometry, table):
    return geometry[..., :3, None] + geometry[..., 3:4, None] * table


def matern(left, right):
    squared = jnp.zeros((), jnp.float32)
    for axis_number in range(3):
        difference = left[..., axis_number, :, None] - right[..., axis_number, None, :]
        squared = squared + difference * difference
    distance = jnp.sqrt(squared)
    decay_rate = root_three / length_scale
    return (1.0 + decay_rate * distance) * jnp.exp(-decay_rate * distance)


def couple_rows(target_geom, source_point_rows, table):
    coeff_width = RANK * RHS
    target_nodes = place_nodes(target_geom, table)
    source_nodes = place_nodes(source_point_rows[..., coeff_width:], table)
    source_coeff = source_point_rows[..., :coeff_width].reshape(
        source_point_rows.shape[:-1] + (RANK, RHS)
    )
    coupling = matern(target_nodes[:, None], source_nodes)
    return jnp.einsum("njkm,njmr->nkr", coupling, source_coeff, precision=exact_product)


def on_device(
    points,
    rhs,
    counts,
    basis,
    leaf_geom,
    leaf_partners,
    leaf_middle_owner,
    leaf_basis_transfer,
    mid_geom,
    mid_parent,
    mid_transfer,
    mid_peers,
    mid_slots,
    top_geom,
    top_offsets,
):
    leaf_count = counts.shape[0]
    mid_count = mid_transfer.shape[0]
    coeff_width = RANK * RHS
    table = node_table()
    position = jnp.arange(PTS, dtype=jnp.int32)
    present = (position[None, :] < counts[:, None]).astype(jnp.float32)
    masked = rhs.reshape(RHS, leaf_count, PTS) * present[None]
    stacked = jnp.concatenate([masked.reshape(RHS, leaf_count * PTS), points], axis=0)
    padded = extended(stacked, (("leaf", 1),), REACH * PTS)
    grid = padded.reshape(RHS + 3, leaf_count + 2 * REACH, PTS)
    leaf_coefficient_rows = jnp.einsum("lpk,rlp->lkr", basis, masked, precision=exact_product)
    leaf_rows = jnp.concatenate(
        [leaf_coefficient_rows.reshape(leaf_count, coeff_width), leaf_geom], axis=1
    )
    leaf_padded = extended(leaf_rows, (("leaf", 0),), REACH)
    members = (
        leaf_middle_owner[0][None, :] == jnp.arange(mid_count, dtype=jnp.int32)[:, None]
    ).astype(jnp.float32)
    upward_coefficients = jnp.einsum(
        "qcz,qct->qzt", leaf_basis_transfer, leaf_coefficient_rows, precision=exact_product
    )
    coeff_mid = jnp.einsum("ml,ljr->mjr", members, upward_coefficients, precision=exact_product)
    mid_rows = jnp.concatenate([coeff_mid.reshape(mid_count, coeff_width), mid_geom], axis=1)
    top_members = (mid_parent[0][None, :] == jnp.arange(TOP, dtype=jnp.int32)[:, None]).astype(
        jnp.float32
    )
    raised = jnp.einsum("mkj,mkr->mjr", mid_transfer, coeff_mid, precision=exact_product)
    partial_top = jnp.einsum("tm,mjr->tjr", top_members, raised, precision=exact_product)
    coeff_top = lax.psum(partial_top, "leaf")
    top_rows = jnp.concatenate([coeff_top.reshape(TOP, coeff_width), top_geom], axis=1)
    top_all = lax.all_gather(top_rows, "group", axis=0, tiled=True)
    total_tops = top_all.shape[0]
    targets = lax.axis_index("group") * TOP + jnp.arange(TOP, dtype=jnp.int32)
    top_source = (targets[:, None] + top_offsets) % total_tops
    local_top = couple_rows(top_geom, top_all[top_source], table)
    mid_all = lax.all_gather(mid_rows, "leaf", axis=0, tiled=True)
    mid_source = mid_peers * mid_count + mid_slots
    source_point_rows = mid_all[mid_source]
    device_middle_index = jnp.einsum(
        "mkj,mjr->mkr", mid_transfer, local_top[mid_parent[0]], precision=exact_product
    )
    device_middle_index = device_middle_index + couple_rows(mid_geom, source_point_rows, table)
    leaf_index = jnp.arange(leaf_count, dtype=jnp.int32)
    far_ids = leaf_index[:, None] + REACH + leaf_partners[:, NEAR:]
    local_leaf = jnp.einsum(
        "ghw,gwt->ght",
        leaf_basis_transfer,
        device_middle_index[leaf_middle_owner[0]],
        precision=exact_product,
    )
    local_leaf = local_leaf + couple_rows(leaf_geom, leaf_padded[far_ids], table)
    far_product = jnp.einsum("lpk,lkr->rlp", basis, local_leaf, precision=exact_product)
    point_cloud = points.reshape(3, leaf_count, PTS)

    def near_block(block_start):
        block_leaves = block_start * 8 + jnp.arange(8, dtype=jnp.int32)
        offsets = lax.dynamic_slice_in_dim(leaf_partners[:, :NEAR], block_start * 8, 8, 0)
        partner = block_leaves[:, None] + REACH + offsets
        target_cloud = point_cloud[:, block_leaves].transpose(1, 0, 2)
        source = grid[:, partner]
        kernel = matern(target_cloud[:, None], source[RHS:].transpose(1, 2, 0, 3))
        return jnp.einsum("bjpq,rbjq->rbp", kernel, source[:RHS], precision=exact_product)

    near_blocks = lax.map(near_block, jnp.arange(leaf_count // 8, dtype=jnp.int32))
    near_product = near_blocks.transpose(1, 0, 2, 3).reshape(RHS, leaf_count, PTS)
    product = (far_product + near_product) * present[None]
    return product.reshape(RHS, leaf_count * PTS)


def solution(mesh):
    placed = (
        P(None, ("group", "leaf")),
        P(None, ("group", "leaf")),
        P(("group", "leaf")),
        P(("group", "leaf"), None, None),
        P(("group", "leaf"), None),
        P(("group", "leaf"), None),
        P(("group", "leaf"), None),
        P(("group", "leaf"), None, None),
        P(("group", "leaf"), None),
        P("group", "leaf"),
        P(("group", "leaf"), None, None),
        P(("group", "leaf"), None),
        P(("group", "leaf"), None),
        P("group", None),
        P("group", None),
    )
    return jax.shard_map(
        on_device, mesh=mesh, in_specs=placed, out_specs=P(None, ("group", "leaf")), check_vma=False
    )
```

profile of v0, /device:TPU:32, one launch (start us, length us, event | category | flops | bytes accessed | tf_op | source)
XLA Modules:
  0.0 284.0 jit_solution(18294623102038642720)
XLA Ops:
  0.0 0.8 fusion.125
  1.0 1.4 fusion.117
  2.7 0.8 copy.62
  3.4 3.4 %collective-permute-start = (f32[16,516]{1,0:T(8,128)S(1)}, f32[16,516]{1,0:T(8,128)}, u32[]{:S(2)}, u32[]{:S(2)}) collective-permute-start(f32[16,516]{1,0:T(8,128)S(1)} %pad_maximum_fusion.4), channel_id=1, source_target_pairs={{0,1},{1,2},{2,3},{3,4},{4,5},{5,6},{6,7},{7,8},{8,9},{9,10},{10,1... | collective-permute-start | bytes 99080 | tf_op jit(solution)/shard_map/ppermute | solution.py:22
  6.8 4.6 %collective-permute-start.1 = (f32[16,516]{1,0:T(8,128)S(1)}, f32[16,516]{1,0:T(8,128)}, u32[]{:S(2)}, u32[]{:S(2)}) collective-permute-start(f32[16,516]{1,0:T(8,128)S(1)} %pad_maximum_fusion.4), channel_id=1, source_target_pairs={{1,0},{2,1},{3,2},{4,3},{5,4},{6,5},{7,6},{8,7},{9,8},{10,9},{11,1... | collective-permute-start | bytes 99080 | tf_op jit(solution)/shard_map/ppermute | solution.py:25
  11.4 0.7 lt.115
  12.2 0.9 broadcast_multiply_fusion
  13.1 0.8 pad_maximum_fusion.1
  13.9 1.9 collective-permute-start.2
  15.8 6.0 %collective-permute-start.3 = (f32[19,2048]{1,0:T(8,128)S(1)}, f32[19,2048]{1,0:T(8,128)S(1)}, u32[]{:S(2)}, u32[]{:S(2)}) collective-permute-start(f32[19,2048]{1,0:T(8,128)S(1)} %pad_maximum_fusion.1), channel_id=1, source_target_pairs={{1,0},{2,1},{3,2},{4,3},{5,4},{6,5},{7,6},{8,7},{9,8},{10,9},{11,1... | collective-permute-start | bytes 466952 | tf_op jit(solution)/shard_map/ppermute | solution.py:25
  21.9 1.3 convolution_bitcast_fusion.2
  23.2 0.9 fusion.119
  24.2 1.3 convolution_bitcast_fusion.5
  25.5 1.0 fusion.121
  26.8 135.6 %psum.7 = f32[16,512]{1,0:T(8,128)S(1)} all-reduce(f32[16,512]{1,0:T(8,128)S(1)} %reshape.345), channel_id=1, replica_groups=mesh['group'=8,'leaf'=32] {'leaf'}, use_global_device_ids=true, to_apply=%region_0.1 | all-reduce | flops 8192 | bytes 65536 | tf_op jit(solution)/shard_map/psum | solution.py:109
  162.4 0.8 copy.52
  163.2 13.4 %all_gather.6 = f32[128,516]{1,0:T(8,128)S(1)} all-gather(f32[16,516]{1,0:T(8,128)S(1)} %pad_maximum_fusion.3), channel_id=1, replica_groups=mesh['group'=8,'leaf'=32] {'group'}, dimensions={0}, use_global_device_ids=true | all-gather | bytes 297216 | tf_op jit(solution)/shard_map/all_gather | solution.py:111
  176.8 1.1 gather_fusion.2
  178.3 54.6 %all_gather.7 = f32[256,516]{1,0:T(8,128)S(1)} all-gather(f32[8,516]{1,0:T(8,128)S(1)} %pad_maximum_fusion.5), channel_id=1, replica_groups=mesh['group'=8,'leaf'=32] {'leaf'}, dimensions={0}, use_global_device_ids=true | all-gather | bytes 544896 | tf_op jit(solution)/shard_map/all_gather | solution.py:116
  233.1 0.7 gather_fusion.4
  235.2 2.7 reshape.346
  239.6 11.0 %fusion.74 = f32[16,32,16]{1,2,0:T(8,128)S(1)} fusion(f32[16,16,32,16]{3,2,1,0:T(8,128)} %reshape.346, f32[16,16,32]{2,1,0:T(8,128)S(1)} %get-tuple-element.63, f32[16,32]{1,0:T(8,128)} %get-tuple-element.72, f32[16,16,32]{2,1,0:T(8,128)S(1)} %get-tuple-element.64, f32[16,32]{1,0:T(8,128)} %get-tuple-element.73, f32[16,16,32]{2,1,0:T(8,128)S(1)} %get-tuple-element.62, ...), kind=kOutput, calls=%fused_computation.83 | convolution fusion | flops 53477376 | bytes 661504 | tf_op jit(solution)/shard_map/njkm,njmr->nkr/dot_general | solution.py:61
  251.1 2.4 convolution_bitcast_fusion.3
  254.5 0.8 pad_maximum_fusion.2
  255.3 0.8 gather_fusion.6
  256.7 0.7 slice_bitcast_fusion.6
  257.4 0.7 reshape.350
  258.1 5.7 %fusion.81 = f32[16,32,16]{1,2,0:T(8,128)S(1)} fusion(f32[16,8,32,16]{3,2,1,0:T(8,128)S(1)} %reshape.350, f32[16,8,32]{2,1,0:T(8,128)} %get-tuple-element.66, f32[16,32]{1,0:T(8,128)S(1)} %get-tuple-element.75, f32[16,8,32]{2,1,0:T(8,128)} %get-tuple-element.67, f32[16,32]{1,0:T(8,128)} %get-tuple-element.76, f32[16,8,32]{2,1,0:T(8,128)} %get-tuple-element.65, ...), kind=kOutput, calls=%fused_computation.91 | convolution fusion | flops 26738688 | bytes 350208 | tf_op jit(solution)/shard_map/njkm,njmr->nkr/dot_general | solution.py:61
  264.7 18.2 %while.10 = (s32[]{:T(128)}, f32[2,16,8,128]{3,1,2,0:T(8,128)S(1)}, s32[2]{0:T(128)S(1)}, s32[16,16]{1,0:T(8,128)S(1)}, f32[19,48,128]{2,0,1:T(8,128)S(1)}, /*in...) while((s32[]{:T(128)}, f32[2,16,8,128]{3,1,2,0:T(8,128)S(1)}, ...), condition=%wide.region_2.3_spmd, body=%wide.region_1.2_spmd.sunk | while | flops 213911856 | bytes 2398031 | solution.py:144
  267.8 6.2 %fusion.187 = f32[2,16,8,128]{3,1,2,0:T(8,128)S(1)} fusion(f32[2,16,8,128]{3,1,2,0:T(8,128)S(1)} %get-tuple-element.144, s32[]{:T(128)} %get-tuple-element.143, f32[8,8,128]{2,1,0:T(8,128)S(1)} %bitcast.200, f32[8,128]{1,0:T(8,128)S(1)} %bitcast.208, f32[8,8,128]{2,1,0:T(8,128)S(1)} %bitcast.201, f32[8,128]{1,0:T(8,128)S(1)} %bitcast.209, ...), kind=kOutput, calls=%fused_computation.32.clone.1 | convolution fusion | flops 213909504 | bytes 700420 | tf_op jit(solution)/shard_map/while/body/eval_jaxpr/bjpq,rbjq->rbp/dot_general | solution.py:142
  276.8 6.2 %fusion.187 = f32[2,16,8,128]{3,1,2,0:T(8,128)S(1)} fusion(f32[2,16,8,128]{3,1,2,0:T(8,128)S(1)} %get-tuple-element.144, s32[]{:T(128)} %get-tuple-element.143, f32[8,8,128]{2,1,0:T(8,128)S(1)} %bitcast.200, f32[8,128]{1,0:T(8,128)S(1)} %bitcast.208, f32[8,8,128]{2,1,0:T(8,128)S(1)} %bitcast.201, f32[8,128]{1,0:T(8,128)S(1)} %bitcast.209, ...), kind=kOutput, calls=%fused_computation.32.clone.1 | convolution fusion | flops 213909504 | bytes 700420 | tf_op jit(solution)/shard_map/while/body/eval_jaxpr/bjpq,rbjq->rbp/dot_general | solution.py:142
  283.3 0.7 copy.92
  (125 shorter events, 12.1 us)
Async XLA Ops:
  0.0 1.0 copy-start
  0.0 176.6 %copy-start.9 = (s32[16,16]{1,0:T(8,128)S(1)}, s32[16,16]{1,0:T(8,128)}, u32[]{:S(2)}) copy-start(s32[16,16]{1,0:T(8,128)} %param.31) | copy-start | bytes 3076
  3.4 251.0 %collective-permute-start = (f32[16,516]{1,0:T(8,128)S(1)}, f32[16,516]{1,0:T(8,128)}, u32[]{:S(2)}, u32[]{:S(2)}) collective-permute-start(f32[16,516]{1,0:T(8,128)S(1)} %pad_maximum_fusion.4), channel_id=1, source_target_pairs={{0,1},{1,2},{2,3},{3,4},{4,5},{5,6},{6,7},{7,8},{8,9},{9,10},{10,1... | collective-permute-start | bytes 99080 | tf_op jit(solution)/shard_map/ppermute | solution.py:22
  6.8 247.6 %collective-permute-start.1 = (f32[16,516]{1,0:T(8,128)S(1)}, f32[16,516]{1,0:T(8,128)}, u32[]{:S(2)}, u32[]{:S(2)}) collective-permute-start(f32[16,516]{1,0:T(8,128)S(1)} %pad_maximum_fusion.4), channel_id=1, source_target_pairs={{1,0},{2,1},{3,2},{4,3},{5,4},{6,5},{7,6},{8,7},{9,8},{10,9},{11,1... | collective-permute-start | bytes 99080 | tf_op jit(solution)/shard_map/ppermute | solution.py:25
  13.9 250.5 %collective-permute-start.2 = (f32[19,2048]{1,0:T(8,128)S(1)}, f32[19,2048]{1,0:T(8,128)S(1)}, u32[]{:S(2)}, u32[]{:S(2)}) collective-permute-start(f32[19,2048]{1,0:T(8,128)S(1)} %pad_maximum_fusion.1), channel_id=1, source_target_pairs={{0,1},{1,2},{2,3},{3,4},{4,5},{5,6},{6,7},{7,8},{8,9},{9,10},{10,1... | collective-permute-start | bytes 466952 | tf_op jit(solution)/shard_map/ppermute | solution.py:22
  15.8 248.6 %collective-permute-start.3 = (f32[19,2048]{1,0:T(8,128)S(1)}, f32[19,2048]{1,0:T(8,128)S(1)}, u32[]{:S(2)}, u32[]{:S(2)}) collective-permute-start(f32[19,2048]{1,0:T(8,128)S(1)} %pad_maximum_fusion.1), channel_id=1, source_target_pairs={{1,0},{2,1},{3,2},{4,3},{5,4},{6,5},{7,6},{8,7},{9,8},{10,9},{11,1... | collective-permute-start | bytes 466952 | tf_op jit(solution)/shard_map/ppermute | solution.py:25
  24.1 153.9 %copy-start.6 = (f32[16,4]{0,1:T(4,128)S(1)}, f32[16,4]{0,1:T(4,128)}, u32[]{:S(2)}) copy-start(f32[16,4]{0,1:T(4,128)} %param.21) | copy-start | bytes 772
  24.1 153.9 %copy-start.7 = (f32[16,4]{0,1:T(4,128)S(1)}, f32[16,4]{0,1:T(4,128)}, u32[]{:S(2)}) copy-start(f32[16,4]{0,1:T(4,128)} %param.30) | copy-start | bytes 772
  26.6 151.5 %copy-start.12 = (s32[1,8]{1,0:T(1,128)S(1)}, s32[1,8]{1,0:T(1,128)}, u32[]{:S(2)}) copy-start(s32[1,8]{1,0:T(1,128)} %param.26) | copy-start | bytes 100
  26.7 151.6 %copy-start.8 = (f32[8,4]{0,1:T(4,128)S(1)}, f32[8,4]{0,1:T(4,128)}, u32[]{:S(2)}) copy-start(f32[8,4]{0,1:T(4,128)} %param.25) | copy-start | bytes 388
  176.6 56.4 %copy-start.10 = (s32[8,8]{1,0:T(8,128)S(1)}, s32[8,8]{1,0:T(8,128)}, u32[]{:S(2)}) copy-start(s32[8,8]{1,0:T(8,128)} %param.29) | copy-start | bytes 772
  176.6 56.4 %copy-start.11 = (s32[8,8]{1,0:T(8,128)S(1)}, s32[8,8]{1,0:T(8,128)}, u32[]{:S(2)}) copy-start(s32[8,8]{1,0:T(8,128)} %param.28) | copy-start | bytes 772
  176.8 57.1 %copy-start.13 = (s32[1,16]{1,0:T(1,128)S(1)}, s32[1,16]{1,0:T(1,128)}, u32[]{:S(2)}) copy-start(s32[1,16]{1,0:T(1,128)} %param.23) | copy-start | bytes 196
  233.8 5.0 %copy-start.5 = (s32[16,16]{1,0:T(8,128)S(1)}, s32[16,16]{1,0:T(8,128)}, u32[]{:S(2)}) copy-start(s32[16,16]{1,0:T(8,128)} %param.22) | copy-start | bytes 3076
  250.5 3.0 %copy-start.2 = (f32[8,32,32]{2,1,0:T(8,128)S(1)}, f32[8,32,32]{2,1,0:T(8,128)}, u32[]{:S(2)}) copy-start(f32[8,32,32]{2,1,0:T(8,128)} %param.27) | copy-start | bytes 98308
  258.1 5.7 %copy-start.1 = (f32[16,32,32]{2,1,0:T(8,128)S(1)}, f32[16,32,32]{2,1,0:T(8,128)}, u32[]{:S(2)}) copy-start(f32[16,32,32]{2,1,0:T(8,128)} %param.24) | copy-start | bytes 196612
  258.1 6.2 %copy-start.3 = (f32[3,2048]{1,0:T(4,128)S(1)}, f32[3,2048]{1,0:T(4,128)}, u32[]{:S(2)}) copy-start(f32[3,2048]{1,0:T(4,128)} %param.17) | copy-start | bytes 73732
  263.8 1.0 copy-start.4
where the time goes:
time: 285 us; the launch traced here: 284 us
  blocking collectives  204 us (72%)
  matrix products  38.4 us (13%)
  local copies, waits for them, and re-layouts  19.3 us (7%)
  starting transfers between devices  15.9 us (6%)
  other arithmetic  4.5 us (2%)
    psum x1, blocking collectives, on_device(): coeff_top = lax.psum(partial_top, 'leaf')  136 us
    all_gather x1, blocking collectives, on_device(): mid_all = lax.all_gather(mid_rows, 'leaf', axis=0, tiled=True)  54.6 us
    dot_general x3, matrix products, couple_rows(): jnp.einsum('njkm,njmr->nkr', coupling, source_coeff, precision=exact_prod...  19 us
    all_gather x1, blocking collectives, on_device(): top_all = lax.all_gather(top_rows, 'group', axis=0, tiled=True)  13.4 us
    dot_general x2, matrix products, near_block(): jnp.einsum('bjpq,rbjq->rbp', kernel, source[:RHS], precision=exact_product)  12.4 us
    ppermute x2, starting transfers between devices, extended(): lax.ppermute(lax.slice_in_dim(block, 0, width, axis=dim), axis, backward)  10.6 us
  transfers between devices with their start and end apart: 4, of which 0 were waited for; matrix products, arithmetic and copies ran while one was open for 14% of the time, Pallas kernels for 0%

commit v1 on v0

--- a/solution.py
+++ b/solution.py
@@ -106,7 +106,11 @@
     )
     raised = jnp.einsum("mkj,mkr->mjr", mid_transfer, coeff_mid, precision=exact_product)
     partial_top = jnp.einsum("tm,mjr->tjr", top_members, raised, precision=exact_product)
-    coeff_top = lax.psum(partial_top, "leaf")
+    coeff_top = partial_top
+    for hop in (1, 2, 4, 8, 16):
+        coeff_top = coeff_top + lax.ppermute(
+            coeff_top, "leaf", [(dev, dev ^ hop) for dev in range(32)]
+        )
     top_rows = jnp.concatenate([coeff_top.reshape(TOP, coeff_width), top_geom], axis=1)
     top_all = lax.all_gather(top_rows, "group", axis=0, tiled=True)
     total_tops = top_all.shape[0]

time: 285 us -> 169 us (0.59)
  blocking collectives: 204 us -> 66.2 us
  waiting for transfers between devices: 0.01 us -> 8.01 us
  starting transfers between devices: 15.9 us -> 23.6 us
    psum x1 -> x0, blocking collectives: 136 us -> none  [on_device(): coeff_top = lax.psum(partial_top, 'leaf')]
    ppermute x0 -> x5, waiting for transfers between devices: none -> 8 us  [on_device(): lax.ppermute(coeff_top, 'leaf', [(dev, dev ^ hop) for dev in range(32)])]
    ppermute x0 -> x5, starting transfers between devices: none -> 7.71 us  [on_device(): lax.ppermute(coeff_top, 'leaf', [(dev, dev ^ hop) for dev in range(32)])]
  transfers between devices with their start and end apart: 4 -> 9, of which waited for: 0 -> 2; matrix products, arithmetic and copies ran while one was open for 14% -> 26% of each run, Pallas kernels for 0% -> 0%
where the time goes in v1:
time: 169 us; the launch traced here: 166 us
  blocking collectives  66.2 us (39%)
  matrix products  39.2 us (23%)
  starting transfers between devices  23.6 us (14%)
  local copies, waits for them, and re-layouts  20.2 us (12%)
  waiting for transfers between devices  8.01 us (5%)
  other arithmetic  6.64 us (4%)
    all_gather x1, blocking collectives, on_device(): mid_all = lax.all_gather(mid_rows, 'leaf', axis=0, tiled=True)  52.5 us
    dot_general x3, matrix products, couple_rows(): jnp.einsum('njkm,njmr->nkr', coupling, source_coeff, precision=exact_prod...  19.8 us
    all_gather x1, blocking collectives, on_device(): top_all = lax.all_gather(top_rows, 'group', axis=0, tiled=True)  13.7 us
    dot_general x2, matrix products, near_block(): jnp.einsum('bjpq,rbjq->rbp', kernel, source[:RHS], precision=exact_product)  12.4 us
    ppermute x2, starting transfers between devices, extended(): lax.ppermute(lax.slice_in_dim(block, 0, width, axis=dim), axis, backward)  10.6 us
    ppermute x5, waiting for transfers between devices, on_device(): lax.ppermute(coeff_top, 'leaf', [(dev, dev ^ hop) for dev in range(32)])  8 us
    ppermute x5, starting transfers between devices, on_device(): lax.ppermute(coeff_top, 'leaf', [(dev, dev ^ hop) for dev in range(32)])  7.71 us
    ppermute x2, starting transfers between devices, extended(): lax.ppermute(lax.slice_in_dim(block, block.shape[dim] - width, None, axis...  5.31 us
  transfers between devices with their start and end apart: 9, of which 2 were waited for; matrix products, arithmetic and copies ran while one was open for 26% of the time, Pallas kernels for 0%

profile of v1, /device:TPU:32, one launch (start us, length us, event | category | flops | bytes accessed | tf_op | source)
XLA Modules:
  0.0 165.9 jit_solution(4247423650059504646)
XLA Ops:
  0.1 0.9 fusion.125
  1.0 1.4 fusion.117
  2.8 0.8 copy.62
  3.5 3.4 %collective-permute-start.5 = (f32[16,516]{1,0:T(8,128)S(1)}, f32[16,516]{1,0:T(8,128)S(1)}, u32[]{:S(2)}, u32[]{:S(2)}) collective-permute-start(f32[16,516]{1,0:T(8,128)S(1)} %pad_maximum_fusion.4), channel_id=1, source_target_pairs={{0,1},{1,2},{2,3},{3,4},{4,5},{5,6},{6,7},{7,8},{8,9},{9,10},{10,1... | collective-permute-start | bytes 99080 | tf_op jit(solution)/shard_map/ppermute | solution.py:22
  6.9 4.6 %collective-permute-start.6 = (f32[16,516]{1,0:T(8,128)S(1)}, f32[16,516]{1,0:T(8,128)S(1)}, u32[]{:S(2)}, u32[]{:S(2)}) collective-permute-start(f32[16,516]{1,0:T(8,128)S(1)} %pad_maximum_fusion.4), channel_id=1, source_target_pairs={{1,0},{2,1},{3,2},{4,3},{5,4},{6,5},{7,6},{8,7},{9,8},{10,9},{11,1... | collective-permute-start | bytes 99080 | tf_op jit(solution)/shard_map/ppermute | solution.py:25
  12.2 0.9 broadcast_multiply_fusion
  13.2 0.8 pad_maximum_fusion.1
  13.9 1.9 %collective-permute-start.7 = (f32[19,2048]{1,0:T(8,128)S(1)}, f32[19,2048]{1,0:T(8,128)S(1)}, u32[]{:S(2)}, u32[]{:S(2)}) collective-permute-start(f32[19,2048]{1,0:T(8,128)S(1)} %pad_maximum_fusion.1), channel_id=1, source_target_pairs={{0,1},{1,2},{2,3},{3,4},{4,5},{5,6},{6,7},{7,8},{8,9},{9,10},{10,1... | collective-permute-start | bytes 466952 | tf_op jit(solution)/shard_map/ppermute | solution.py:22
  15.9 6.0 %collective-permute-start.8 = (f32[19,2048]{1,0:T(8,128)S(1)}, f32[19,2048]{1,0:T(8,128)S(1)}, u32[]{:S(2)}, u32[]{:S(2)}) collective-permute-start(f32[19,2048]{1,0:T(8,128)S(1)} %pad_maximum_fusion.1), channel_id=1, source_target_pairs={{1,0},{2,1},{3,2},{4,3},{5,4},{6,5},{7,6},{8,7},{9,8},{10,9},{11,1... | collective-permute-start | bytes 466952 | tf_op jit(solution)/shard_map/ppermute | solution.py:25
  21.9 1.3 convolution_bitcast_fusion.2
  23.2 0.9 fusion.119
  24.2 1.3 convolution_bitcast_fusion.5
  25.4 1.0 fusion.121
  28.1 0.8 copy.57
  28.9 52.5 %all_gather.7 = f32[256,516]{1,0:T(8,128)S(1)} all-gather(f32[8,516]{1,0:T(8,128)S(1)} %pad_maximum_fusion.5), channel_id=1, replica_groups=mesh['group'=8,'leaf'=32] {'leaf'}, dimensions={0}, use_global_device_ids=true | all-gather | bytes 544896 | tf_op jit(solution)/shard_map/all_gather | solution.py:120
  86.1 3.1 %convolution_bitcast_fusion.3 = f32[8,32,16]{1,2,0:T(8,128)} fusion(f32[8,8,32,16]{3,2,1,0:T(8,128)S(1)} %reshape.348, f32[8,8,32]{2,1,0:T(8,128)S(1)} %get-tuple-element.69, f32[8,32]{1,0:T(8,128)S(1)} %get-tuple-element.78, f32[8,8,32]{2,1,0:T(8,128)S(1)} %get-tuple-element.70, f32[8,32]{1,0:T(8,128)S(1)} %get-tuple-element.79, ...), kind=kOutput, calls=%fused_computation.92 | convolution fusion | flops 13369344 | bytes 175104 | tf_op jit(solution)/shard_map/njkm,njmr->nkr/dot_general | solution.py:61
  89.3 1.6 collective-permute-start.1
  90.9 0.8 gather_fusion.6
  92.3 3.5 %collective-permute-done.1 = f32[16,32,16]{1,0,2:T(8,128)S(1)} collective-permute-done((f32[16,32,16]{1,0,2:T(8,128)S(1)}, f32[16,32,16]{1,0,2:T(8,128)S(1)}, u32[]{:S(2)}, u32[]{:S(2)}) %collective-permute-start.1) | collective-permute-done | bytes 32800 | tf_op jit(solution)/shard_map/ppermute | solution.py:111
  95.9 0.9 collective-permute-start.2
  98.3 4.5 %collective-permute-done.2 = f32[16,32,16]{1,0,2:T(8,128)} collective-permute-done((f32[16,32,16]{1,0,2:T(8,128)S(1)}, f32[16,32,16]{1,0,2:T(8,128)}, u32[]{:S(2)}, u32[]{:S(2)}) %collective-permute-start.2) | collective-permute-done | bytes 32800 | tf_op jit(solution)/shard_map/ppermute | solution.py:111
  102.7 0.9 add.346
  103.7 3.0 %collective-permute-start.3 = (f32[16,32,16]{1,0,2:T(8,128)S(1)}, f32[16,32,16]{1,0,2:T(8,128)S(1)}, u32[]{:S(2)}, u32[]{:S(2)}) collective-permute-start(f32[16,32,16]{1,0,2:T(8,128)S(1)} %add.346), channel_id=1, source_target_pairs={{0,8},{1,9},{2,10},{3,11},{4,12},{5,13},{6,14},{7,15},{8,0},{9,1},... | collective-permute-start | bytes 98312 | tf_op jit(solution)/shard_map/ppermute | solution.py:111
  106.7 5.8 %fusion.81 = f32[16,32,16]{1,2,0:T(8,128)S(1)} fusion(f32[16,8,32,16]{3,2,1,0:T(8,128)S(1)} %reshape.350, f32[16,8,32]{2,1,0:T(8,128)} %get-tuple-element.66, f32[16,32]{1,0:T(8,128)} %get-tuple-element.75, f32[16,8,32]{2,1,0:T(8,128)} %get-tuple-element.67, f32[16,32]{1,0:T(8,128)} %get-tuple-element.76, f32[16,8,32]{2,1,0:T(8,128)} %get-tuple-element.65, ...), kind=kOutput, calls=%fused_computation.91 | convolution fusion | flops 26738688 | bytes 350208 | tf_op jit(solution)/shard_map/njkm,njmr->nkr/dot_general | solution.py:61
  112.5 2.0 %collective-permute-start.4 = (f32[16,32,16]{1,0,2:T(8,128)S(1)}, f32[16,32,16]{1,0,2:T(8,128)S(1)}, u32[]{:S(2)}, u32[]{:S(2)}) collective-permute-start(f32[16,32,16]{1,0,2:T(8,128)S(1)} %add.347), channel_id=1, source_target_pairs={{0,16},{1,17},{2,18},{3,19},{4,20},{5,21},{6,22},{7,23},{8,24},{9,... | collective-permute-start | bytes 98312 | tf_op jit(solution)/shard_map/ppermute | solution.py:111
  115.0 18.0 %while.10 = (s32[]{:T(128)}, f32[2,16,8,128]{3,1,2,0:T(8,128)S(1)}, s32[2]{0:T(128)S(1)}, s32[16,16]{1,0:T(8,128)S(1)}, f32[19,48,128]{2,0,1:T(8,128)S(1)}, /*in...) while((s32[]{:T(128)}, f32[2,16,8,128]{3,1,2,0:T(8,128)S(1)}, ...), condition=%wide.region_1.2_spmd, body=%wide.region_0.1_spmd.sunk | while | flops 213911856 | bytes 2398031 | solution.py:148
  117.8 6.2 %fusion.187 = f32[2,16,8,128]{3,1,2,0:T(8,128)S(1)} fusion(f32[2,16,8,128]{3,1,2,0:T(8,128)S(1)} %get-tuple-element.144, s32[]{:T(128)} %get-tuple-element.143, f32[8,8,128]{2,1,0:T(8,128)S(1)} %bitcast.200, f32[8,128]{1,0:T(8,128)S(1)} %bitcast.208, f32[8,8,128]{2,1,0:T(8,128)S(1)} %bitcast.201, f32[8,128]{1,0:T(8,128)S(1)} %bitcast.209, ...), kind=kOutput, calls=%fused_computation.32.clone.1 | convolution fusion | flops 213909504 | bytes 700420 | tf_op jit(solution)/shard_map/while/body/eval_jaxpr/bjpq,rbjq->rbp/dot_general | solution.py:146
  126.8 6.2 %fusion.187 = f32[2,16,8,128]{3,1,2,0:T(8,128)S(1)} fusion(f32[2,16,8,128]{3,1,2,0:T(8,128)S(1)} %get-tuple-element.144, s32[]{:T(128)} %get-tuple-element.143, f32[8,8,128]{2,1,0:T(8,128)S(1)} %bitcast.200, f32[8,128]{1,0:T(8,128)S(1)} %bitcast.208, f32[8,8,128]{2,1,0:T(8,128)S(1)} %bitcast.201, f32[8,128]{1,0:T(8,128)S(1)} %bitcast.209, ...), kind=kOutput, calls=%fused_computation.32.clone.1 | convolution fusion | flops 213909504 | bytes 700420 | tf_op jit(solution)/shard_map/while/body/eval_jaxpr/bjpq,rbjq->rbp/dot_general | solution.py:146
  133.3 13.7 %all_gather.6 = f32[128,516]{1,0:T(8,128)S(1)} all-gather(f32[16,516]{1,0:T(8,128)S(1)} %pad_maximum_fusion.3), channel_id=1, replica_groups=mesh['group'=8,'leaf'=32] {'group'}, dimensions={0}, use_global_device_ids=true | all-gather | bytes 297216 | tf_op jit(solution)/shard_map/all_gather | solution.py:115
  147.0 1.1 gather_fusion.2
  148.9 2.8 %reshape.346 = f32[16,16,32,16]{3,2,1,0:T(8,128)} reshape(f32[16,16,512]{2,1,0:T(8,128)S(1)} %slice.202) | data formatting | bytes 1048576 | tf_op jit(solution)/shard_map/reshape | solution.py:57
  151.7 10.9 %fusion.74 = f32[16,32,16]{1,2,0:T(8,128)S(1)} fusion(f32[16,16,32,16]{3,2,1,0:T(8,128)} %reshape.346, f32[16,16,32]{2,1,0:T(8,128)S(1)} %get-tuple-element.63, f32[16,32]{1,0:T(8,128)S(1)} %get-tuple-element.72, f32[16,16,32]{2,1,0:T(8,128)S(1)} %get-tuple-element.64, f32[16,32]{1,0:T(8,128)S(1)} %copy-done.11, f32[16,16,32]{2,1,0:T(8,128)S(1)} %get-tuple-element.62, ...), kind=kOutput, calls=%fused_computation.83 | convolution fusion | flops 53477376 | bytes 661504 | tf_op jit(solution)/shard_map/njkm,njmr->nkr/dot_general | solution.py:61
  (141 shorter events, 18.4 us)
Async XLA Ops:
  0.0 1.0 copy-start
  0.0 82.6 %copy-start.7 = (f32[16,4]{0,1:T(4,128)S(1)}, f32[16,4]{0,1:T(4,128)}, u32[]{:S(2)}) copy-start(f32[16,4]{0,1:T(4,128)} %param.21) | copy-start | bytes 772
  0.0 82.3 %copy-start.14 = (s32[1,16]{1,0:T(1,128)S(1)}, s32[1,16]{1,0:T(1,128)}, u32[]{:S(2)}) copy-start(s32[1,16]{1,0:T(1,128)} %param.23) | copy-start | bytes 196
  0.0 82.3 %copy-start.9 = (f32[8,4]{0,1:T(4,128)S(1)}, f32[8,4]{0,1:T(4,128)}, u32[]{:S(2)}) copy-start(f32[8,4]{0,1:T(4,128)} %param.25) | copy-start | bytes 388
  0.0 81.4 %copy-start.13 = (s32[8,8]{1,0:T(8,128)S(1)}, s32[8,8]{1,0:T(8,128)}, u32[]{:S(2)}) copy-start(s32[8,8]{1,0:T(8,128)} %param.28) | copy-start | bytes 772
  0.0 81.4 %copy-start.12 = (s32[8,8]{1,0:T(8,128)S(1)}, s32[8,8]{1,0:T(8,128)}, u32[]{:S(2)}) copy-start(s32[8,8]{1,0:T(8,128)} %param.29) | copy-start | bytes 772
  0.0 82.3 %copy-start.10 = (s32[16,16]{1,0:T(8,128)S(1)}, s32[16,16]{1,0:T(8,128)}, u32[]{:S(2)}) copy-start(s32[16,16]{1,0:T(8,128)} %param.31) | copy-start | bytes 3076
  0.1 82.5 %copy-start.8 = (f32[16,4]{0,1:T(4,128)S(1)}, f32[16,4]{0,1:T(4,128)}, u32[]{:S(2)}) copy-start(f32[16,4]{0,1:T(4,128)} %param.30) | copy-start | bytes 772
  0.1 85.2 %copy-start.5 = (s32[16,16]{1,0:T(8,128)S(1)}, s32[16,16]{1,0:T(8,128)}, u32[]{:S(2)}) copy-start(s32[16,16]{1,0:T(8,128)} %param.22) | copy-start | bytes 3076
  3.5 87.4 %collective-permute-start.5 = (f32[16,516]{1,0:T(8,128)S(1)}, f32[16,516]{1,0:T(8,128)S(1)}, u32[]{:S(2)}, u32[]{:S(2)}) collective-permute-start(f32[16,516]{1,0:T(8,128)S(1)} %pad_maximum_fusion.4), channel_id=1, source_target_pairs={{0,1},{1,2},{2,3},{3,4},{4,5},{5,6},{6,7},{7,8},{8,9},{9,10},{10,1... | collective-permute-start | bytes 99080 | tf_op jit(solution)/shard_map/ppermute | solution.py:22
  6.9 84.0 %collective-permute-start.6 = (f32[16,516]{1,0:T(8,128)S(1)}, f32[16,516]{1,0:T(8,128)S(1)}, u32[]{:S(2)}, u32[]{:S(2)}) collective-permute-start(f32[16,516]{1,0:T(8,128)S(1)} %pad_maximum_fusion.4), channel_id=1, source_target_pairs={{1,0},{2,1},{3,2},{4,3},{5,4},{6,5},{7,6},{8,7},{9,8},{10,9},{11,1... | collective-permute-start | bytes 99080 | tf_op jit(solution)/shard_map/ppermute | solution.py:25
  13.9 100.6 %collective-permute-start.7 = (f32[19,2048]{1,0:T(8,128)S(1)}, f32[19,2048]{1,0:T(8,128)S(1)}, u32[]{:S(2)}, u32[]{:S(2)}) collective-permute-start(f32[19,2048]{1,0:T(8,128)S(1)} %pad_maximum_fusion.1), channel_id=1, source_target_pairs={{0,1},{1,2},{2,3},{3,4},{4,5},{5,6},{6,7},{7,8},{8,9},{9,10},{10,1... | collective-permute-start | bytes 466952 | tf_op jit(solution)/shard_map/ppermute | solution.py:22
  15.9 98.7 %collective-permute-start.8 = (f32[19,2048]{1,0:T(8,128)S(1)}, f32[19,2048]{1,0:T(8,128)S(1)}, u32[]{:S(2)}, u32[]{:S(2)}) collective-permute-start(f32[19,2048]{1,0:T(8,128)S(1)} %pad_maximum_fusion.1), channel_id=1, source_target_pairs={{1,0},{2,1},{3,2},{4,3},{5,4},{6,5},{7,6},{8,7},{9,8},{10,9},{11,1... | collective-permute-start | bytes 466952 | tf_op jit(solution)/shard_map/ppermute | solution.py:25
  26.4 62.8 %collective-permute-start = (f32[16,32,16]{1,0,2:T(8,128)S(1)}, f32[16,32,16]{1,0,2:T(8,128)S(1)}, u32[]{:S(2)}, u32[]{:S(2)}) collective-permute-start(f32[16,32,16]{1,0,2:T(8,128)S(1)} %fusion.121), channel_id=1, source_target_pairs={{0,1},{1,0},{2,3},{3,2},{4,5},{5,4},{6,7},{7,6},{8,9},{9,8},{10,11... | collective-permute-start | bytes 98312 | tf_op jit(solution)/shard_map/ppermute | solution.py:111
  89.3 6.6 %collective-permute-start.1 = (f32[16,32,16]{1,0,2:T(8,128)S(1)}, f32[16,32,16]{1,0,2:T(8,128)S(1)}, u32[]{:S(2)}, u32[]{:S(2)}) collective-permute-start(f32[16,32,16]{1,0,2:T(8,128)S(1)} %add.344), channel_id=1, source_target_pairs={{0,2},{1,3},{2,0},{3,1},{4,6},{5,7},{6,4},{7,5},{8,10},{9,11},{10,... | collective-permute-start | bytes 98312 | tf_op jit(solution)/shard_map/ppermute | solution.py:111
  95.9 6.9 %collective-permute-start.2 = (f32[16,32,16]{1,0,2:T(8,128)S(1)}, f32[16,32,16]{1,0,2:T(8,128)}, u32[]{:S(2)}, u32[]{:S(2)}) collective-permute-start(f32[16,32,16]{1,0,2:T(8,128)S(1)} %add.345), channel_id=1, source_target_pairs={{0,4},{1,5},{2,6},{3,7},{4,0},{5,1},{6,2},{7,3},{8,12},{9,13},{10,... | collective-permute-start | bytes 98312 | tf_op jit(solution)/shard_map/ppermute | solution.py:111
  98.3 16.3 %copy-start.3 = (f32[3,2048]{1,0:T(4,128)S(1)}, f32[3,2048]{1,0:T(4,128)}, u32[]{:S(2)}) copy-start(f32[3,2048]{1,0:T(4,128)} %param.17) | copy-start | bytes 73732
  103.7 8.9 %collective-permute-start.3 = (f32[16,32,16]{1,0,2:T(8,128)S(1)}, f32[16,32,16]{1,0,2:T(8,128)S(1)}, u32[]{:S(2)}, u32[]{:S(2)}) collective-permute-start(f32[16,32,16]{1,0,2:T(8,128)S(1)} %add.346), channel_id=1, source_target_pairs={{0,8},{1,9},{2,10},{3,11},{4,12},{5,13},{6,14},{7,15},{8,0},{9,1},... | collective-permute-start | bytes 98312 | tf_op jit(solution)/shard_map/ppermute | solution.py:111
  112.5 2.5 %copy-start.4 = (f32[2,16,8,128]{3,1,2,0:T(8,128)S(1)}, f32[2,16,8,128]{3,1,2,0:T(8,128)}, u32[]{:S(2)}) copy-start(f32[2,16,8,128]{3,1,2,0:T(8,128)} %custom-call.14) | copy-start | bytes 393220
  112.5 20.4 %collective-permute-start.4 = (f32[16,32,16]{1,0,2:T(8,128)S(1)}, f32[16,32,16]{1,0,2:T(8,128)S(1)}, u32[]{:S(2)}, u32[]{:S(2)}) collective-permute-start(f32[16,32,16]{1,0,2:T(8,128)S(1)} %add.347), channel_id=1, source_target_pairs={{0,16},{1,17},{2,18},{3,19},{4,20},{5,21},{6,22},{7,23},{8,24},{9,... | collective-permute-start | bytes 98312 | tf_op jit(solution)/shard_map/ppermute | solution.py:111
  148.1 3.6 %copy-start.11 = (f32[16,32]{1,0:T(8,128)S(1)}, f32[16,32]{1,0:T(8,128)}, u32[]{:S(2)}) copy-start(f32[16,32]{1,0:T(8,128)} %get-tuple-element.73) | copy-start | bytes 6148
  151.7 11.6 %copy-start.2 = (f32[8,32,32]{2,1,0:T(8,128)S(1)}, f32[8,32,32]{2,1,0:T(8,128)}, u32[]{:S(2)}) copy-start(f32[8,32,32]{2,1,0:T(8,128)} %param.27) | copy-start | bytes 98308
  151.7 11.6 %copy-start.6 = (f32[8,32,16]{1,2,0:T(8,128)S(1)}, f32[8,32,16]{1,2,0:T(8,128)}, u32[]{:S(2)}) copy-start(f32[8,32,16]{1,2,0:T(8,128)} %convolution_bitcast_fusion.3) | copy-start | bytes 49156
  151.7 12.7 %copy-start.1 = (f32[16,32,32]{2,1,0:T(8,128)S(1)}, f32[16,32,32]{2,1,0:T(8,128)}, u32[]{:S(2)}) copy-start(f32[16,32,32]{2,1,0:T(8,128)} %param.24) | copy-start | bytes 196612
